TPU v7x, 128 devices: a whole 4x4x4 slice. The times are simulated.
128 devices in a mesh: scan: 16 (over z_lo, x, core), tgt: 8 (over y, z_hi).
Axes of the slice: x: 4, y: 4, z: 4 (z_hi: 2, z_lo: 2; z = z_hi * 2 + z_lo), core: 2. Of those that a mesh axis runs over, the one named last changes fastest.
Arguments:
- series: bfloat16 [96, 1200, 8192], P('scan', None, 'tgt'), as said below
- seed_index: int32 [512], replicated, may hold values from 0 to 8191
Outputs:
- affinity: bfloat16 [8192, 8192], P('tgt', 'scan')
Inputs may be any that keep to these rules, and one draw needn't show every extreme that they name: No grayordinate's series is constant over the frames of a scan.
All inputs are finite; a program needn't handle non-finite values.
Results may differ from a plain program's by a relative error of at most 0.0034.
Values may be sent and summed in bfloat16 or wider, within the bound.
A program may use at most 128 MiB of HBM per device.

v0:
```python
import jax
import jax.numpy as jnp
from jax import lax
from jax.sharding import PartitionSpec as P

epsilon = 1e-06
clip_level = 0.95
capacity = 96


def fisher_sum(correl):
    clipped = jnp.clip(correl, -clip_level, clip_level)
    above = jnp.prod(1.0 + clipped, axis=0)
    below = jnp.prod(1.0 - clipped, axis=0)
    return 0.5 * jnp.log(above / below)


def normalize_columns(profile):
    center = jnp.mean(profile, axis=0)
    deviate = profile - center
    spread = jnp.mean(deviate * deviate, axis=0)
    return (deviate * lax.rsqrt(spread + epsilon)).astype(jnp.bfloat16)


def body(series, seed_index):
    frame_count = series.shape[1]
    local_width = series.shape[2]
    seed_count = seed_index.shape[0]
    tgt_size = lax.axis_size("tgt")
    scan_size = lax.axis_size("scan")
    whole_width = local_width * tgt_size
    me = lax.axis_index("tgt")
    owner = seed_index // local_width
    local_seed = seed_index - owner * local_width
    owned = owner[:, None] == jnp.arange(tgt_size)[None, :]
    before = jnp.cumsum(owned.astype(jnp.int32), axis=0)
    count = before[-1]
    rank = jnp.sum(jnp.where(owned, before, 0), axis=1) - 1
    values = series.astype(jnp.float32)
    center = jnp.mean(values, axis=1, keepdims=True)
    deviate = values - center
    spread = jnp.mean(deviate * deviate, axis=1, keepdims=True)
    standard = (deviate * lax.rsqrt(spread + epsilon)).astype(jnp.bfloat16)

    def correlate(seed_cols):
        correl = jnp.einsum("sfk,sfg->skg", seed_cols, standard, preferred_element_type=jnp.float32)
        return fisher_sum(correl / frame_count)

    def packed():
        mine = (owner == me)[:, None] & (rank[:, None] == jnp.arange(capacity)[None, :])
        column = jnp.sum(jnp.where(mine, local_seed[:, None] + 1, 0), axis=0) - 1
        pick = (jnp.arange(local_width)[:, None] == column[None, :]).astype(jnp.bfloat16)
        picked = jnp.einsum(
            "sfg,gk->sfk", standard, pick, preferred_element_type=jnp.float32
        ).astype(jnp.bfloat16)
        seed_cols = lax.all_gather(picked, "tgt", axis=2, tiled=True)
        return jnp.take(correlate(seed_cols), owner * capacity + rank, axis=0)

    def general():
        inside = owner == me
        picked = jnp.take(standard, local_seed, axis=2)
        picked = jnp.where(inside[None, None, :], picked, jnp.zeros_like(picked))
        return correlate(lax.psum(picked, "tgt"))

    running = lax.cond(jnp.max(count) <= capacity, packed, general)
    part = lax.psum_scatter(running, "scan", scatter_dimension=1, tiled=True)
    row_prof = lax.all_gather(normalize_columns(part), "scan", axis=1, tiled=True)
    col_width = whole_width // scan_size
    spot = lax.axis_index("scan") * col_width
    start = spot % local_width
    col_prof = lax.dynamic_slice_in_dim(row_prof, start, col_width, 1)
    col_prof = jnp.where(spot // local_width == me, col_prof, jnp.zeros_like(col_prof))
    col_prof = lax.psum(col_prof, "tgt")
    product = jnp.dot(row_prof.T, col_prof, preferred_element_type=jnp.float32)
    return jnp.tanh(product / seed_count).astype(jnp.bfloat16)


def solution(mesh):
    in_specs = (P("scan", None, "tgt"), P())
    out_specs = P("tgt", "scan")
    return jax.shard_map(body, mesh=mesh, in_specs=in_specs, out_specs=out_specs, check_vma=False)
```

profile of v0, /device:TPU:0, one launch (start us, length us, event | category | flops | bytes accessed | tf_op | source)
XLA Modules:
  0.0 424.0 jit_solution(14349586945426796302)
XLA Ops:
  7.4 0.7 multiply_subtract_fusion
  8.1 1.1 reduce-window.6
  9.2 0.2 slice_reduce_fusion
  9.5 0.1 add_bitcast_fusion
  9.5 8.8 %convert_reduce_fusion = f32[6,1024]{1,0:T(8,128)S(1)} fusion(bf16[6,1200,1024]{2,1,0:T(8,128)(2,1)} %param.4), kind=kLoop, calls=%fused_computation.32 | loop fusion | flops 14739456 | bytes 14770176 | tf_op jit(solution)/shard_map/reduce_sum | solution.py:40
  18.3 9.0 %fusion.7 = f32[6,1024]{1,0:T(8,128)S(1)} fusion(bf16[6,1200,1024]{2,1,0:T(8,128)(2,1)} %param.4, f32[6,1024]{1,0:T(8,128)S(1)} %broadcast_multiply_fusion), kind=kLoop, calls=%fused_computation.35 | loop fusion | flops 29485056 | bytes 14794752 | tf_op jit(solution)/shard_map/reduce_sum | solution.py:42
  27.4 11.7 %fusion.8 = bf16[6,1200,1024]{2,1,0:T(8,128)(2,1)} fusion(bf16[6,1200,1024]{2,1,0:T(8,128)(2,1)} %param.4, f32[6,1024]{1,0:T(8,128)S(1)} %add_rsqrt_fusion, f32[6,1024]{1,0:T(8,128)S(1)} %broadcast_multiply_fusion), kind=kLoop, calls=%fused_computation.36 | loop fusion | flops 29491200 | bytes 29540352 | tf_op jit(solution)/shard_map/convert_element_type | solution.py:43
  39.1 0.7 slice_reduce_fusion.1
  40.5 185.9 %conditional.1 = (f32[512,1024]{1,0:T(8,128)S(1)}) conditional(s32[]{:T(128)} %convert_element_type.28, (s32[]{:T(128)}, s32[512]{0:T(512)S(1)}, s32[512]{0:T(512)S(1)}, bf16[6,1200,1024]{2,1,0:T(8,128)(2,1)}) %tuple.11, (s32[512]{0:T(512)S(1)}, s32[512,8]{0,1:T(8,128)S(1)}, s32[512,8]{0,1:T(8,128)S(1)}, s32[512]{0:T(512)S(1)}, s32[]{:T(128)}, ...), branch_computations={%region_5.9_spmd, %region_9.14_spmd} | conditional | flops 12770038784 | bytes 150587424 | solution.py:65
  40.7 0.0 all-gather.3.cloned.1.call-start
  40.8 0.1 select_reduce_fusion
  41.0 10.8 %fusion = bf16[6,1200,96]{1,2,0:T(8,128)(2,1)} fusion(bf16[6,1200,1024]{2,1,0:T(8,128)(2,1)} %get-tuple-element.49, s32[96]{0:T(128)S(1)} %broadcast_add_fusion.1), kind=kOutput, calls=%fused_computation.16 | convolution fusion | flops 1416367104 | bytes 16128384 | tf_op jit(solution)/shard_map/cond/branch_1_fun/sfg,gk->sfk/dot_general | solution.py:53
  51.8 0.0 all-gather.3.cloned.1.call-update
  51.9 142.9 %all-gather.3.cloned.1.call-done = bf16[6,1200,768]{1,2,0:T(8,128)(2,1)} async-done(((bf16[6,1200,96]{1,2,0:T(8,128)(2,1)}), bf16[6,1200,768]{1,2,0:T(8,128)(2,1)}) %all-gather.3.cloned.1.call-update) | async-done | bytes 11059216 | tf_op jit(solution)/shard_map/cond/branch_1_fun/all_gather | solution.py:56
  194.7 23.5 %subtract_reduce_fusion.1 = (f32[768,1024]{1,0:T(8,128)}, f32[768,1024]{1,0:T(8,128)}) fusion(bf16[6,1200,768]{1,2,0:T(8,128)(2,1)} %all-gather.3.cloned.1.call-done, bf16[6,1200,1024]{2,1,0:T(8,128)(2,1)} %get-tuple-element.49), kind=kOutput, calls=%fused_computation.11 | convolution fusion | flops 11351359488 | bytes 32096256 | tf_op jit(solution)/shard_map/cond/branch_1_fun/sfk,sfg->skg/dot_general | solution.py:46
  218.2 3.7 log_multiply_fusion.1
  221.9 2.7 gather_fusion.1
  224.6 1.8 broadcast_select_fusion
  226.4 0.0 reduce-scatter.4.cloned.1.call-start
  226.4 1.9 copy.18
  228.3 0.0 reduce-scatter.4.cloned.1.call-update
  228.3 0.0 all-gather.5.cloned.1.call-start
  228.4 61.9 %reduce-scatter.4.cloned.1.call-done = f32[64,512]{1,0:T(8,128)} async-done(((f32[1024,512]{1,0:T(8,128)}), f32[64,512]{1,0:T(8,128)}) %reduce-scatter.4.cloned.1.call-update) | async-done | bytes 131088
  290.3 1.0 bitcast_reduce_fusion
  291.3 1.1 multiply_reduce_fusion
  292.4 1.6 multiply_convert_fusion
  294.0 0.0 all-gather.5.cloned.1.call-update
  294.1 0.0 all-reduce.5.cloned.1.call-start
  294.1 31.1 %all-gather.5.cloned.1.call-done = bf16[512,1024]{0,1:T(8,128)(2,1)} async-done(((bf16[512,64]{0,1:T(8,128)(2,1)}), bf16[512,1024]{0,1:T(8,128)(2,1)}) %all-gather.5.cloned.1.call-update) | async-done | bytes 1048592 | tf_op jit(solution)/shard_map/all_gather | solution.py:67
  325.2 1.9 dynamic-slice_select_fusion
  327.2 0.0 all-reduce.5.cloned.1.call-update
  327.2 86.1 %all-reduce.5.cloned.1.call-done = bf16[512,512]{0,1:T(8,128)(2,1)} async-done(((bf16[512,512]{0,1:T(8,128)(2,1)}), bf16[512,512]{0,1:T(8,128)(2,1)}) %all-reduce.5.cloned.1.call-update) | async-done | bytes 524304 | tf_op jit(solution)/shard_map/psum | solution.py:73
  413.3 3.1 tanh_convert_fusion
  (14 shorter events, 0.1 us)
Async XLA Ops:
  40.7 154.0 %all-gather.3.cloned.1.call-start = ((), (), s32[]{:S(2)}) async-start(), calls=%async_computation.2 | async-start | bytes 13271040 | tf_op jit(solution)/shard_map/cond/branch_1_fun/all_gather | solution.py:56
  226.4 63.9 %reduce-scatter.4.cloned.1.call-start = ((), (), s32[]{:S(2)}) async-start(), calls=%async_computation.5 | async-start | bytes 2228224
  228.3 96.9 %all-gather.5.cloned.1.call-start = ((), (), s32[]{:S(2)}) async-start(), calls=%async_computation.3 | async-start | bytes 1114112 | tf_op jit(solution)/shard_map/all_gather | solution.py:67
  294.1 119.2 %all-reduce.5.cloned.1.call-start = ((), (), s32[]{:S(2)}) async-start(), calls=%async_computation.4 | async-start | bytes 1048576 | tf_op jit(solution)/shard_map/psum | solution.py:73
Sparse Core Ops, SparseCore 0:
  52.0 142.6 all-gather.2
Sparse Core Ops, SparseCore 1:
  229.2 61.0 reduce-scatter.3
  294.1 31.0 all-gather.4
  327.6 85.7 all-reduce.4
where the time goes:
time: 424 us
  waiting for transfers between devices  322 us (76%)
  other arithmetic  43.5 us (10%)
  matrix products  37.4 us (9%)
  between operations  15.8 us (4%)
  local copies, waits for them, and re-layouts  4.82 us (1%)
    all_gather x1, waiting for transfers between devices, packed(): seed_cols = lax.all_gather(picked, 'tgt', axis=2, tiled=True)  143 us
    psum x1, waiting for transfers between devices, body(): col_prof = lax.psum(col_prof, 'tgt')  86.1 us
    unnamed x4, waiting for transfers between devices  61.9 us
    all_gather x1, waiting for transfers between devices, body(): lax.all_gather(normalize_columns(part), 'scan', axis=1, tiled=True)  31.1 us
    dot_general x1, matrix products, correlate(): jnp.einsum('sfk,sfg->skg', seed_cols, standard, preferred_element_type=jn...  23.5 us
    convert_element_type x1, other arithmetic, body(): standard = (deviate * lax.rsqrt(spread + epsilon)).astype(jnp.bfloat16)  11.7 us
    dot_general x1, matrix products, packed(): jnp.einsum('sfg,gk->sfk', standard, pick, preferred_element_type=jnp.floa...  10.8 us
    reduce_sum x1, other arithmetic, body(): spread = jnp.mean(deviate * deviate, axis=1, keepdims=True)  9.04 us
  transfers between devices with their start and end apart: 4, of which 4 were waited for; matrix products, arithmetic and copies ran while one was open for 0% of the time, Pallas kernels for 0%

commit v1 on v0

--- a/solution.py
+++ b/solution.py
@@ -6,6 +6,12 @@
 epsilon = 1e-06
 clip_level = 0.95
 capacity = 96
+cut_files = lambda s0, bus_axis: jnp.concatenate(
+    jax.lax.all_to_all(
+        jnp.stack([s0 for _ in range(jax.lax.axis_size(bus_axis))], axis=0), bus_axis, 0, 0
+    ),
+    axis=2,
+)
 
 
 def fisher_sum(correl):
@@ -53,7 +59,7 @@
         picked = jnp.einsum(
             "sfg,gk->sfk", standard, pick, preferred_element_type=jnp.float32
         ).astype(jnp.bfloat16)
-        seed_cols = lax.all_gather(picked, "tgt", axis=2, tiled=True)
+        seed_cols = cut_files(picked, "tgt")
         return jnp.take(correlate(seed_cols), owner * capacity + rank, axis=0)
 
     def general():

time: 424 us -> 467 us (1.10)
  waiting for transfers between devices: 322 us -> 342 us
  local copies, waits for them, and re-layouts: 4.82 us -> 20.7 us
  starting transfers between devices: 0.17 us -> 8 us
    all_to_all x0 -> x1, waiting for transfers between devices: none -> 161 us  [jax.lax.all_to_all(jnp.stack([s0 for _ in range(jax.lax.axis_size(bus_axi...]
    all_gather x1 -> x0, waiting for transfers between devices: 143 us -> none  [packed(): seed_cols = lax.all_gather(picked, 'tgt', axis=2, tiled=True)]
    reshape x0 -> x1, local copies, waits for them, and re-layouts: none -> 10.1 us  [jnp.concatenate(jax.lax.all_to_all(jnp.stack([s0 for _ in range(jax.lax.a...]
    all_to_all x0 -> x1, starting transfers between devices: none -> 7.86 us  [jax.lax.all_to_all(jnp.stack([s0 for _ in range(jax.lax.axis_size(bus_axi...]
    another operation x2 -> x3, local copies, waits for them, and re-layouts: 0.01 us -> 5.81 us  [the longest x1 5.8 us: jnp.stack([s0 for _ in range(jax.lax.axis_size(bus_axis))], axis=0)]
where the time goes in v1:
time: 467 us
  waiting for transfers between devices  342 us (73%)
  other arithmetic  43.5 us (9%)
  matrix products  36.2 us (8%)
  local copies, waits for them, and re-layouts  20.7 us (4%)
  between operations  15.8 us (3%)
  starting transfers between devices  8 us (2%)
    all_to_all x1, waiting for transfers between devices, jax.lax.all_to_all(jnp.stack([s0 for _ in range(jax.lax.axis_size(bus_axi...  161 us
    psum x1, waiting for transfers between devices, body(): col_prof = lax.psum(col_prof, 'tgt')  86.1 us
    unnamed x4, waiting for transfers between devices  63.9 us
    all_gather x1, waiting for transfers between devices, body(): lax.all_gather(normalize_columns(part), 'scan', axis=1, tiled=True)  31.1 us
    dot_general x1, matrix products, correlate(): jnp.einsum('sfk,sfg->skg', seed_cols, standard, preferred_element_type=jn...  23.5 us
    convert_element_type x1, other arithmetic, body(): standard = (deviate * lax.rsqrt(spread + epsilon)).astype(jnp.bfloat16)  11.7 us
    reshape x1, local copies, waits for them, and re-layouts, jnp.concatenate(jax.lax.all_to_all(jnp.stack([s0 for _ in range(jax.lax.a...  10.1 us
    dot_general x1, matrix products, packed(): jnp.einsum('sfg,gk->sfk', standard, pick, preferred_element_type=jnp.floa...  9.65 us
  transfers between devices with their start and end apart: 4, of which 4 were waited for; matrix products, arithmetic and copies ran while one was open for 0% of the time, Pallas kernels for 0%

profile of v1, /device:TPU:0, one launch (start us, length us, event | category | flops | bytes accessed | tf_op | source)
XLA Modules:
  0.0 466.9 jit_solution(17587957959107857154)
XLA Ops:
  7.4 0.7 multiply_subtract_fusion
  8.1 1.1 reduce-window.6
  9.2 0.2 slice_reduce_fusion
  9.5 0.1 add_bitcast_fusion
  9.5 8.8 %convert_reduce_fusion = f32[6,1024]{1,0:T(8,128)S(1)} fusion(bf16[6,1200,1024]{2,1,0:T(8,128)(2,1)} %param.4), kind=kLoop, calls=%fused_computation.32 | loop fusion | flops 14739456 | bytes 14770176 | tf_op jit(solution)/shard_map/reduce_sum | solution.py:46
  18.3 9.0 %fusion.7 = f32[6,1024]{1,0:T(8,128)S(1)} fusion(bf16[6,1200,1024]{2,1,0:T(8,128)(2,1)} %param.4, f32[6,1024]{1,0:T(8,128)S(1)} %broadcast_multiply_fusion), kind=kLoop, calls=%fused_computation.35 | loop fusion | flops 29485056 | bytes 14794752 | tf_op jit(solution)/shard_map/reduce_sum | solution.py:48
  27.4 11.7 %fusion.8 = bf16[6,1200,1024]{2,1,0:T(8,128)(2,1)} fusion(bf16[6,1200,1024]{2,1,0:T(8,128)(2,1)} %param.4, f32[6,1024]{1,0:T(8,128)S(1)} %add_rsqrt_fusion, f32[6,1024]{1,0:T(8,128)S(1)} %broadcast_multiply_fusion), kind=kLoop, calls=%fused_computation.36 | loop fusion | flops 29491200 | bytes 29540352 | tf_op jit(solution)/shard_map/convert_element_type | solution.py:49
  39.1 0.7 slice_reduce_fusion.1
  40.5 226.9 %conditional.1 = (f32[512,1024]{1,0:T(8,128)S(1)}) conditional(s32[]{:T(128)} %convert_element_type.28, (s32[]{:T(128)}, s32[512]{0:T(512)S(1)}, s32[512]{0:T(512)S(1)}, bf16[6,1200,1024]{2,1,0:T(8,128)(2,1)}) %tuple.11, (s32[512]{0:T(512)S(1)}, s32[512,8]{0,1:T(8,128)S(1)}, s32[512,8]{0,1:T(8,128)S(1)}, s32[512]{0:T(512)S(1)}, s32[]{:T(128)}, ...), branch_computations={%region_5.9_spmd, %region_9.14_spmd} | conditional | flops 12770038784 | bytes 150587424 | solution.py:71
  40.8 0.1 select_reduce_fusion
  40.9 9.7 %fusion = bf16[6,1200,96]{1,2,0:T(8,128)(2,1)S(1)} fusion(bf16[6,1200,1024]{2,1,0:T(8,128)(2,1)} %get-tuple-element.49, s32[96]{0:T(128)S(1)} %broadcast_add_fusion.1), kind=kOutput, calls=%fused_computation.16 | convolution fusion | flops 1416367104 | bytes 16128384 | tf_op jit(solution)/shard_map/cond/branch_1_fun/sfg,gk->sfk/dot_general | solution.py:59
  50.6 5.8 %stack.0 = bf16[8,6,1200,96]{2,3,1,0:T(8,128)(2,1)} broadcast(bf16[6,1200,96]{1,2,0:T(8,128)(2,1)S(1)} %fusion), dimensions={1,2,3} | broadcast | bytes 12441600 | tf_op jit(solution)/shard_map/cond/branch_1_fun/stack | solution.py:11
  56.4 7.9 %all-to-all-start = ((bf16[8,6,1200,96]{2,3,1,0:T(8,128)(2,1)}), bf16[8,6,1200,96]{2,3,1,0:T(8,128)(2,1)}, u32[]{:S(2)}, u32[]{:S(2)}) async-start(bf16[8,6,1200,96]{2,3,1,0:T(8,128)(2,1)} %stack.0), calls=%async_computation | async-start | bytes 23592960 | tf_op jit(solution)/shard_map/cond/branch_1_fun/all_to_all | solution.py:10
  64.3 161.4 %all-to-all-done = bf16[8,6,1200,96]{2,3,1,0:T(8,128)(2,1)} async-done(((bf16[8,6,1200,96]{2,3,1,0:T(8,128)(2,1)}), bf16[8,6,1200,96]{2,3,1,0:T(8,128)(2,1)}, u32[]{:S(2)}, u32[]{:S(2)}) %all-to-all-start) | async-done | bytes 11059232 | tf_op jit(solution)/shard_map/cond/branch_1_fun/all_to_all | solution.py:10
  225.7 10.1 %copy.22 = bf16[6,1200,8,96]{1,3,2,0:T(8,128)(2,1)} copy(bf16[6,1200,8,96]{1,3,0,2:T(8,128)(2,1)} %bitcast.3) | data formatting | bytes 22118400 | tf_op jit(solution)/shard_map/cond/branch_1_fun/reshape | solution.py:9
  235.7 23.5 %subtract_reduce_fusion.1 = (f32[768,1024]{1,0:T(8,128)}, f32[768,1024]{1,0:T(8,128)}) fusion(bf16[6,1200,768]{1,2,0:T(8,128)(2,1)} %bitcast.29, bf16[6,1200,1024]{2,1,0:T(8,128)(2,1)} %get-tuple-element.49), kind=kOutput, calls=%fused_computation.11 | convolution fusion | flops 11351359488 | bytes 32096256 | tf_op jit(solution)/shard_map/cond/branch_1_fun/sfk,sfg->skg/dot_general | solution.py:52
  259.2 3.7 log_multiply_fusion.1
  262.9 2.7 gather_fusion
  265.6 1.8 broadcast_select_fusion
  267.4 0.0 reduce-scatter.4.cloned.1.call-start
  267.5 1.9 copy.27
  269.4 0.0 reduce-scatter.4.cloned.1.call-update
  269.4 0.0 all-gather.2.cloned.1.call-start
  269.4 63.8 %reduce-scatter.4.cloned.1.call-done = f32[64,512]{1,0:T(8,128)} async-done(((f32[1024,512]{1,0:T(8,128)}), f32[64,512]{1,0:T(8,128)}) %reduce-scatter.4.cloned.1.call-update) | async-done | bytes 131088
  333.2 1.0 bitcast_reduce_fusion
  334.3 1.1 multiply_reduce_fusion
  335.4 1.6 multiply_convert_fusion
  337.0 0.0 all-gather.2.cloned.1.call-update
  337.0 0.0 all-reduce.5.cloned.1.call-start
  337.1 31.1 %all-gather.2.cloned.1.call-done = bf16[512,1024]{0,1:T(8,128)(2,1)} async-done(((bf16[512,64]{0,1:T(8,128)(2,1)}), bf16[512,1024]{0,1:T(8,128)(2,1)}) %all-gather.2.cloned.1.call-update) | async-done | bytes 1048592 | tf_op jit(solution)/shard_map/all_gather | solution.py:73
  368.2 1.9 dynamic-slice_select_fusion
  370.1 0.0 all-reduce.5.cloned.1.call-update
  370.1 86.1 %all-reduce.5.cloned.1.call-done = bf16[512,512]{0,1:T(8,128)(2,1)} async-done(((bf16[512,512]{0,1:T(8,128)(2,1)}), bf16[512,512]{0,1:T(8,128)(2,1)}) %all-reduce.5.cloned.1.call-update) | async-done | bytes 524304 | tf_op jit(solution)/shard_map/psum | solution.py:79
  456.3 3.1 tanh_convert_fusion
  (14 shorter events, 0.1 us)
Async XLA Ops:
  56.4 169.3 %all-to-all-start = ((bf16[8,6,1200,96]{2,3,1,0:T(8,128)(2,1)}), bf16[8,6,1200,96]{2,3,1,0:T(8,128)(2,1)}, u32[]{:S(2)}, u32[]{:S(2)}) async-start(bf16[8,6,1200,96]{2,3,1,0:T(8,128)(2,1)} %stack.0), calls=%async_computation | async-start | bytes 23592960 | tf_op jit(solution)/shard_map/cond/branch_1_fun/all_to_all | solution.py:10
  267.4 65.8 %reduce-scatter.4.cloned.1.call-start = ((), (), s32[]{:S(2)}) async-start(), calls=%async_computation.5 | async-start | bytes 2228224
  269.4 98.8 %all-gather.2.cloned.1.call-start = ((), (), s32[]{:S(2)}) async-start(), calls=%async_computation.3 | async-start | bytes 1114112 | tf_op jit(solution)/shard_map/all_gather | solution.py:73
  337.0 119.2 %all-reduce.5.cloned.1.call-start = ((), (), s32[]{:S(2)}) async-start(), calls=%async_computation.4 | async-start | bytes 1048576 | tf_op jit(solution)/shard_map/psum | solution.py:79
Sparse Core Ops, SparseCore 1:
  270.3 62.9 reduce-scatter.3
  337.1 31.0 all-gather.1
  370.5 85.7 all-reduce.4
